TPU v7x, 32 devices: a whole 2x2x4 slice. The times are simulated.
32 devices in a mesh: rep: 2 (over x), atom: 16 (over z, y, core).
Axes of the slice: x: 2, y: 2, z: 4, core: 2. Of those that a mesh axis runs over, the one named last changes fastest.
Arguments:
- features: bfloat16 [4096, 256], P(('rep', 'atom')), parts along dimension 0, may hold values from -6 to 6
- fractional: float32 [3, 4096], P(None, ('rep', 'atom')), parts along dimension 1, may hold values from 0 to 1, as said below
- distances: float32 [64, 4096], P(None, ('rep', 'atom')), parts along dimension 1, may hold values from 0.8 to 4.8
- neighbours: int32 [64, 4096], P(None, ('rep', 'atom')), parts along dimension 1, may hold values from 0 to 383
- edge_mask: int32 [64, 4096], P(None, ('rep', 'atom')), parts along dimension 1, may hold values 0 or 1
- wave_index: int32 [3, 2048], replicated, may hold values from -6 to 6
- w_rbf: bfloat16 [2, 64, 512], replicated, may hold values from -1.5 to 1.5
- w_filter: bfloat16 [2, 512, 256], replicated, may hold values from -0.25 to 0.25
- w_mixing: bfloat16 [2, 256, 256], replicated, may hold values from -0.375 to 0.375
- w_short: bfloat16 [2, 256, 256], replicated, may hold values from -0.375 to 0.375
- w_long: bfloat16 [2, 256, 256], replicated, may hold values from -0.375 to 0.375
Outputs:
- features_out: bfloat16 [4096, 256], P(('rep', 'atom')), parts along dimension 0
There are 2 independent parts, one for each index of `rep`. A program takes and returns all parts, laid end to end along the dimension named above; an argument that names none is the same for every part. Nothing has to cross between parts.
Inputs may be any that keep to these rules, and one draw needn't show every extreme that they name: neighbours[n, i] indexes the concatenation of the previous brick, atom i's own brick and the next brick, cyclic over the 16 bricks. `fractional`: atom i has its z coordinate within brick i // 128, that is between (i // 128) * 128 / 2048 and one brick further.
All inputs are finite; a program needn't handle non-finite values. No bound on the sum of `edge_mask` on one device may be relied on, other than what follows from the above.
Results may differ from a plain program's by a relative error of at most 0.01.
Values may be sent and summed in bfloat16 or wider, within the bound.
A program may use at most 64 MiB of HBM per device.

v0:
```python
import functools
import math

import jax
import jax.numpy as jnp
import numpy as np
from jax import lax
from jax.experimental import pallas as pl
from jax.experimental.pallas import tpu as pltpu
from jax.sharding import PartitionSpec as P

MOST = 6
STEPS = 8
Z_ROWS = 16


def half_plane():
    pairs = [(0, m1) for m1 in range(MOST + 1)]
    pairs += [(m0, m1) for m0 in range(1, MOST + 1) for m1 in range(-MOST, MOST + 1)]
    return pairs + [(0, 0)] * (-len(pairs) % STEPS)


PAIRS = half_plane()


def row_weights(wave_index, atoms_all):
    m0, m1, m2 = wave_index[0], wave_index[1], wave_index[2]
    flip = (m0 < 0) | ((m0 == 0) & (m1 < 0))
    sign = jnp.where(flip, -1, 1)
    m0, m1, m2 = sign * m0, sign * m1, sign * m2
    pair = jnp.where(m0 == 0, m1, (MOST + 1) + (m0 - 1) * (2 * MOST + 1) + m1 + MOST)
    one_pair = (pair[None, :] == jnp.arange(len(PAIRS))[:, None]).astype(jnp.bfloat16)
    one_z = ((m2 + Z_ROWS // 2)[None, :] == jnp.arange(Z_ROWS)[:, None]).astype(jnp.bfloat16)
    count = lax.dot_general(
        one_pair, one_z, (((1,), (1,)), ((), ())), preferred_element_type=jnp.float32
    )
    grid = np.array(PAIRS, np.float32)
    z = np.arange(Z_ROWS, dtype=np.float32) - Z_ROWS // 2
    norm = (grid * grid).sum(axis=1)[:, None] + (z * z)[None, :]
    weight = count / (1.0 + norm / 16.0) / math.sqrt(atoms_all)
    return jnp.broadcast_to(weight[:, None, :], (len(PAIRS), 2, Z_ROWS)).reshape(-1, 1)


def filter_kernel(layer, distance_ref, rbf_ref, filter_ref, out_ref, rbf_t, filter_t):
    @pl.when(pl.program_id(0) == 0)
    def _():
        rbf_t[...] = (rbf_ref[...].astype(jnp.float32) * 0.5).T.astype(jnp.bfloat16)
        filter_t[...] = filter_ref[...].astype(jnp.float32).T.astype(jnp.bfloat16)

    count = rbf_ref.shape[0]
    slots, rows = distance_ref.shape
    center = 0.5 + 4.5 * lax.broadcasted_iota(jnp.int32, (count, rows), 0).astype(jnp.float32) / (
        count - 1
    )
    parts = []
    for slot in range(slots):
        offset = distance_ref[slot : slot + 1, :] - center
        parts.append(jnp.exp(-4.0 * offset * offset).astype(jnp.bfloat16))
    basis = jnp.concatenate(parts, axis=1)
    half = jnp.dot(rbf_t[...], basis, preferred_element_type=jnp.float32)
    inner = (half + half * jnp.tanh(half)).astype(jnp.bfloat16)
    out_ref[...] = jnp.dot(filter_t[...], inner, preferred_element_type=jnp.float32).astype(
        jnp.bfloat16
    )


def edge_filters(layer, distances, w_rbf, w_filter):
    slots, rows = distances.shape
    _, count, hidden = w_rbf.shape
    width = w_filter.shape[2]
    group = slots // STEPS
    return pl.pallas_call(
        functools.partial(filter_kernel, layer),
        out_shape=jax.ShapeDtypeStruct((width, slots * rows), jnp.bfloat16),
        grid=(STEPS,),
        in_specs=[
            pl.BlockSpec((group, rows), lambda g: (g, 0)),
            pl.BlockSpec((None, count, hidden), lambda g: (layer, 0, 0)),
            pl.BlockSpec((None, hidden, width), lambda g: (layer, 0, 0)),
        ],
        out_specs=pl.BlockSpec((width, group * rows), lambda g: (0, g)),
        scratch_shapes=[
            pltpu.VMEM((hidden, count), jnp.bfloat16),
            pltpu.VMEM((width, hidden), jnp.bfloat16),
        ],
        cost_estimate=pl.CostEstimate(
            flops=2 * slots * rows * hidden * (256 + width),
            bytes_accessed=2 * slots * rows * width,
            transcendentals=slots * rows * hidden,
        ),
        name="filters",
    )(distances, w_rbf, w_filter)


def wave_kernel(fraction_ref, out_ref, plane_c, plane_s, z_c, z_s):
    step = pl.program_id(0)
    atoms = fraction_ref.shape[1]
    tau = 2.0 * math.pi

    @pl.when(step == 0)
    def _():
        def table(axis, count, first):
            order = lax.broadcasted_iota(jnp.int32, (count, atoms), 0) + first
            turn = fraction_ref[axis : axis + 1, :] * order.astype(jnp.float32)
            turn = (turn - jnp.floor(turn + 0.5)) * tau
            return jnp.cos(turn), jnp.sin(turn)

        cos_x, sin_x = table(0, 8, 0)
        cos_y, sin_y = table(1, 16, -8)
        cos_z, sin_z = table(2, Z_ROWS, -(Z_ROWS // 2))
        z_c[...] = cos_z
        z_s[...] = sin_z
        for at, (m0, m1) in enumerate(PAIRS):
            cx, sx = cos_x[m0 : m0 + 1], sin_x[m0 : m0 + 1]
            cy, sy = cos_y[m1 + 8 : m1 + 9], sin_y[m1 + 8 : m1 + 9]
            plane_c[at // 8, at % 8 : at % 8 + 1, :] = cx * cy - sx * sy
            plane_s[at // 8, at % 8 : at % 8 + 1, :] = sx * cy + cx * sy

    group = len(PAIRS) // STEPS
    for local in range(group):
        at = step * group + local
        c = plane_c[at // 8, pl.ds(at % 8, 1), :]
        s = plane_s[at // 8, pl.ds(at % 8, 1), :]
        row = local * 2 * Z_ROWS
        out_ref[row : row + Z_ROWS, :] = (c * z_c[...] - s * z_s[...]).astype(jnp.bfloat16)
        out_ref[row + Z_ROWS : row + 2 * Z_ROWS, :] = (s * z_c[...] + c * z_s[...]).astype(
            jnp.bfloat16
        )


def waves(fraction):
    atoms = fraction.shape[1]
    rows = len(PAIRS) * 2 * Z_ROWS
    block = rows // STEPS
    return pl.pallas_call(
        wave_kernel,
        out_shape=jax.ShapeDtypeStruct((rows, atoms), jnp.bfloat16),
        grid=(STEPS,),
        in_specs=[pl.BlockSpec(fraction.shape, lambda g: (0, 0))],
        out_specs=pl.BlockSpec((block, atoms), lambda g: (g, 0)),
        scratch_shapes=[
            pltpu.VMEM((len(PAIRS) // 8, 8, atoms), jnp.float32),
            pltpu.VMEM((len(PAIRS) // 8, 8, atoms), jnp.float32),
            pltpu.VMEM((Z_ROWS, atoms), jnp.float32),
            pltpu.VMEM((Z_ROWS, atoms), jnp.float32),
        ],
        cost_estimate=pl.CostEstimate(
            flops=6 * rows * atoms, bytes_accessed=2 * rows * atoms, transcendentals=80 * atoms
        ),
        name="waves",
    )(fraction)


def layer_kernel(
    field_scale,
    brick_ref,
    all_ref,
    before_ref,
    own_ref,
    after_ref,
    distance_ref,
    neighbour_ref,
    mask_ref,
    filters_ref,
    wave_ref,
    wave_own_ref,
    weight_ref,
    mixing_ref,
    short_ref,
    long_ref,
    out_ref,
    table,
    message,
    field,
):
    step = pl.program_id(0)
    rows = own_ref.shape[0]

    @pl.when(step == 0)
    def _():
        for at, ref in enumerate((before_ref, own_ref, after_ref)):
            table[:, at * rows : (at + 1) * rows] = ref[...].astype(jnp.float32).T.astype(jnp.bfloat16)
        message[...] = jnp.zeros_like(message)
        field[...] = jnp.zeros_like(field)

    structure = jnp.dot(wave_ref[...], all_ref[...], preferred_element_type=jnp.float32)
    scaled = (structure * weight_ref[...]).astype(jnp.bfloat16)
    potential = jnp.dot(scaled, mixing_ref[...], preferred_element_type=jnp.float32).astype(jnp.bfloat16)
    field[...] += lax.dot_general(
        wave_own_ref[...],
        potential,
        (((0,), (0,)), ((), ())),
        preferred_element_type=jnp.float32,
    )

    weight = 0.5 * (jnp.cos(math.pi * distance_ref[...] / 5.0) + 1.0)
    weight = weight * mask_ref[...].astype(jnp.float32)
    place = lax.broadcasted_iota(jnp.int32, (3 * rows, rows), 0)
    slots = distance_ref.shape[0]
    picks = []
    for slot in range(slots):
        hit = place == neighbour_ref[slot : slot + 1, :]
        picks.append(jnp.where(hit, weight[slot : slot + 1, :], 0.0).astype(jnp.bfloat16))
    pick = jnp.concatenate(picks, axis=1)
    gathered = jnp.dot(table[...], pick, preferred_element_type=jnp.float32)
    product = gathered * filters_ref[...].astype(jnp.float32)
    total = message[...]
    for slot in range(slots):
        total = total + product[:, slot * rows : (slot + 1) * rows]
    message[...] = total

    @pl.when(step == pl.num_programs(0) - 1)
    def _():
        update = jnp.dot(
            message[...].T.astype(jnp.bfloat16), short_ref[...], preferred_element_type=jnp.float32
        )
        update = update + jnp.dot(
            (field[...] * field_scale).astype(jnp.bfloat16),
            long_ref[...],
            preferred_element_type=jnp.float32,
        )
        state = own_ref[...].astype(jnp.float32) + update * jax.nn.sigmoid(update)
        out_ref[...] = state.astype(jnp.bfloat16)


def layer_update(
    layer, brick, bricks, field_scale, everyone, distances, neighbours, mask, filters, wave, weight,
    w_mixing, w_short, w_long,
):
    atoms, width = everyone.shape
    slots, rows = distances.shape
    group = slots // STEPS
    block = wave.shape[0] // STEPS
    slab = pl.BlockSpec((group, rows), lambda g, b: (g, 0))
    matrix = pl.BlockSpec((None, width, width), lambda g, b: (layer, 0, 0))
    return pl.pallas_call(
        functools.partial(layer_kernel, field_scale),
        out_shape=jax.ShapeDtypeStruct((rows, width), jnp.bfloat16),
        grid_spec=pltpu.PrefetchScalarGridSpec(
            num_scalar_prefetch=1,
            grid=(STEPS,),
            in_specs=[
                pl.BlockSpec((atoms, width), lambda g, b: (0, 0)),
                pl.BlockSpec((rows, width), lambda g, b: (lax.rem(b[0] + bricks - 1, bricks), 0)),
                pl.BlockSpec((rows, width), lambda g, b: (b[0], 0)),
                pl.BlockSpec((rows, width), lambda g, b: (lax.rem(b[0] + 1, bricks), 0)),
                slab,
                slab,
                slab,
                pl.BlockSpec((width, group * rows), lambda g, b: (0, g)),
                pl.BlockSpec((block, atoms), lambda g, b: (g, 0)),
                pl.BlockSpec((block, rows), lambda g, b: (g, b[0])),
                pl.BlockSpec((block, 1), lambda g, b: (g, 0)),
                matrix,
                matrix,
                matrix,
            ],
            out_specs=pl.BlockSpec((rows, width), lambda g, b: (0, 0)),
            scratch_shapes=[
                pltpu.VMEM((width, 3 * rows), jnp.bfloat16),
                pltpu.VMEM((width, rows), jnp.float32),
                pltpu.VMEM((rows, width), jnp.float32),
            ],
        ),
        name="update",
    )(
        brick, everyone, everyone, everyone, everyone, distances, neighbours, mask, filters, wave,
        wave, weight, w_mixing, w_short, w_long,
    )


def doubling_gather(block):
    bricks = lax.axis_size("atom")
    index = lax.axis_index("atom")
    held = block[None]
    distance = bricks // 2
    while distance >= 1:
        other = lax.ppermute(held, "atom", [(i, i ^ distance) for i in range(bricks)])
        low = (index // distance) % 2 == 0
        held = jnp.stack([jnp.where(low, held, other), jnp.where(low, other, held)], axis=1)
        held = held.reshape((-1,) + block.shape)
        distance //= 2
    return held


def per_device(
    features, fractional, distances, neighbours, edge_mask, wave_index,
    w_rbf, w_filter, w_mixing, w_short, w_long,
):
    bricks = lax.axis_size("atom")
    brick = jnp.reshape(lax.axis_index("atom"), (1,)).astype(jnp.int32)
    field_scale = 4.0 / math.sqrt(wave_index.shape[1])
    fraction = doubling_gather(fractional).transpose(1, 0, 2).reshape(fractional.shape[0], -1)
    wave = waves(fraction)
    weight = row_weights(wave_index, features.shape[0] * bricks)
    state = features
    for layer in range(w_rbf.shape[0]):
        slots = distances
        if layer > 0:
            slots, state = lax.optimization_barrier((distances, state))
        everyone = doubling_gather(state).reshape(-1, state.shape[1])
        filters = edge_filters(layer, slots, w_rbf, w_filter)
        state = layer_update(
            layer, brick, bricks, field_scale, everyone, distances, neighbours, edge_mask, filters,
            wave, weight, w_mixing, w_short, w_long,
        )
    return state


def solution(mesh):
    split_rows = P(("rep", "atom"), None)
    split_columns = P(None, ("rep", "atom"))
    in_specs = (split_rows,) + (split_columns,) * 4 + (P(),) * 6
    return jax.shard_map(
        per_device, mesh=mesh, in_specs=in_specs, out_specs=split_rows, check_vma=False
    )
```

profile of v0, /device:TPU:0, one launch (start us, length us, event | category | flops | bytes accessed | tf_op | source)
XLA Modules:
  0.0 107.9 jit_solution(13873974577210291058)
XLA Ops:
  0.0 4.1 %collective-permute-start.4 = (f32[1,3,128]{2,1,0:T(4,128)}, f32[1,3,128]{2,1,0:T(4,128)S(1)}, u32[]{:S(2)}, u32[]{:S(2)}) collective-permute-start(f32[1,3,128]{2,1,0:T(4,128)} %bitcast.123), channel_id=1, source_target_pairs={{0,8},{1,9},{2,10},{3,11},{4,12},{5,13},{6,14},{7,15},{8,0},{9,1},... | collective-permute-start | bytes 4616 | tf_op jit(solution)/shard_map/ppermute | solution.py:278
  4.1 0.9 multiply_add_fusion
  5.0 0.9 compare_select_fusion
  5.9 8.3 %filters.2.filters_ref = bf16[256,8192]{1,0:T(8,128)(2,1)} custom-call(f32[64,128]{1,0:T(8,128)} %distance_ref.6, bf16[2,64,512]{2,1,0:T(8,128)(2,1)} %rbf_ref.3, bf16[2,512,256]{2,1,0:T(8,128)(2,1)} %filter_ref.3), custom_call_target="tpu_custom_call" | custom-call | flops 4294967296 | bytes 4194304 | tf_op jit(solution)/shard_map/filters/pallas_call | solution.py:72
  14.2 2.0 %collective-permute-start.5 = (f32[2,3,128]{2,1,0:T(4,128)S(1)}, f32[2,3,128]{2,1,0:T(4,128)S(1)}, u32[]{:S(2)}, u32[]{:S(2)}) collective-permute-start(f32[2,3,128]{2,1,0:T(4,128)S(1)} %maximum_bitcast_fusion.2), channel_id=1, source_target_pairs={{0,4},{1,5},{2,6},{3,7},{4,0},{5,1},{6,2},{7,3},{8,12},{9,13},{10,... | collective-permute-start | bytes 9224 | tf_op jit(solution)/shard_map/ppermute | solution.py:278
  16.4 1.5 %collective-permute-done.5 = f32[2,3,128]{2,1,0:T(4,128)S(1)} collective-permute-done((f32[2,3,128]{2,1,0:T(4,128)S(1)}, f32[2,3,128]{2,1,0:T(4,128)S(1)}, u32[]{:S(2)}, u32[]{:S(2)}) %collective-permute-start.5) | collective-permute-done | bytes 3104 | tf_op jit(solution)/shard_map/ppermute | solution.py:278
  17.9 1.9 %collective-permute-start.6 = (f32[4,3,128]{2,0,1:T(4,128)S(1)}, f32[4,3,128]{2,0,1:T(4,128)S(1)}, u32[]{:S(2)}, u32[]{:S(2)}) collective-permute-start(f32[4,3,128]{2,0,1:T(4,128)S(1)} %bitcast.119), channel_id=1, source_target_pairs={{0,2},{1,3},{2,0},{3,1},{4,6},{5,7},{6,4},{7,5},{8,10},{9,11},{10,... | collective-permute-start | bytes 18440 | tf_op jit(solution)/shard_map/ppermute | solution.py:278
  19.8 1.4 %collective-permute-done.1 = bf16[2,128,256]{2,1,0:T(8,128)(2,1)S(1)} collective-permute-done((bf16[2,128,256]{2,1,0:T(8,128)(2,1)S(1)}, bf16[2,128,256]{2,1,0:T(8,128)(2,1)S(1)}, u32[]{:S(2)}, u32[]{:S(2)}) %collective-permute-start.1) | collective-permute-done | bytes 131104 | tf_op jit(solution)/shard_map/ppermute | solution.py:278
  21.3 1.6 %collective-permute-start.2 = (bf16[4,128,256]{2,1,0:T(8,128)(2,1)S(1)}, bf16[4,128,256]{2,1,0:T(8,128)(2,1)S(1)}, u32[]{:S(2)}, u32[]{:S(2)}) collective-permute-start(bf16[4,128,256]{2,1,0:T(8,128)(2,1)S(1)} %bitcast.111), channel_id=1, source_target_pairs={{0,2},{1,3},{2,0},{3,1},{4,6},{5,7},{6,4},{7,5},{8,10},{9,11},{10,... | collective-permute-start | bytes 786440 | tf_op jit(solution)/shard_map/ppermute | solution.py:278
  23.0 4.7 %collective-permute-done.2 = bf16[4,128,256]{2,1,0:T(8,128)(2,1)S(1)} collective-permute-done((bf16[4,128,256]{2,1,0:T(8,128)(2,1)S(1)}, bf16[4,128,256]{2,1,0:T(8,128)(2,1)S(1)}, u32[]{:S(2)}, u32[]{:S(2)}) %collective-permute-start.2) | collective-permute-done | bytes 262176 | tf_op jit(solution)/shard_map/ppermute | solution.py:278
  28.4 1.9 %reshape.53.weight_ref = f32[2816,1]{1,0:T(8,128)} reshape(f32[88,2,16]{2,1,0:T(2,128)S(1)} %broadcast_in_dim.31) | data formatting | bytes 22528 | tf_op jit(solution)/shard_map/reshape | solution.py:41
  30.3 0.6 copy.54
  30.9 9.4 %waves.1.wave_ref.wave_own_ref = bf16[2816,2048]{1,0:T(8,128)(2,1)} custom-call(f32[3,2048]{1,0:T(4,128)} %bitcast.114), custom_call_target="tpu_custom_call" | custom-call | flops 34603008 | bytes 11534336 | tf_op jit(solution)/shard_map/waves/pallas_call | solution.py:135
  40.5 1.1 copy.42
  41.6 18.1 %update.2 = bf16[128,256]{1,0:T(8,128)(2,1)} custom-call(s32[1]{0:T(128)} %bitcast.brick_ref, bf16[2048,256]{1,0:T(8,128)(2,1)} %bitcast.105, bf16[2048,256]{1,0:T(8,128)(2,1)} %bitcast.106, bf16[2048,256]{1,0:T(8,128)(2,1)} %bitcast.107, bf16[2048,256]{1,0:T(8,128)(2,1)} %bitcast.108, f32[64,128]{1,0:T(8,128)} %distance_ref.6, s32[64,128]{1,0:T(8,128)} %neighbour_ref.3, ...), custom_call_target="tpu_custom_call" | custom-call | tf_op jit(solution)/shard_map/update/pallas_call | solution.py:236
  59.7 2.2 %collective-permute-start.8 = (bf16[1,128,256]{2,1,0:T(8,128)(2,1)}, bf16[1,128,256]{2,1,0:T(8,128)(2,1)S(1)}, u32[]{:S(2)}, u32[]{:S(2)}) collective-permute-start(bf16[1,128,256]{2,1,0:T(8,128)(2,1)} %bitcast.113), channel_id=1, source_target_pairs={{0,8},{1,9},{2,10},{3,11},{4,12},{5,13},{6,14},{7,15},{8,0},{9,1},... | collective-permute-start | bytes 196616 | tf_op jit(solution)/shard_map/ppermute | solution.py:278
  61.8 4.2 %collective-permute-done.8 = bf16[1,128,256]{2,1,0:T(8,128)(2,1)S(1)} collective-permute-done((bf16[1,128,256]{2,1,0:T(8,128)(2,1)}, bf16[1,128,256]{2,1,0:T(8,128)(2,1)S(1)}, u32[]{:S(2)}, u32[]{:S(2)}) %collective-permute-start.8) | collective-permute-done | bytes 65568 | tf_op jit(solution)/shard_map/ppermute | solution.py:278
  66.0 0.9 select_bitcast_fusion.13
  67.0 5.5 %collective-permute-done.9 = bf16[2,128,256]{2,1,0:T(8,128)(2,1)S(1)} collective-permute-done((bf16[2,128,256]{2,1,0:T(8,128)(2,1)S(1)}, bf16[2,128,256]{2,1,0:T(8,128)(2,1)S(1)}, u32[]{:S(2)}, u32[]{:S(2)}) %collective-permute-start.9) | collective-permute-done | bytes 131104 | tf_op jit(solution)/shard_map/ppermute | solution.py:278
  72.6 1.4 %collective-permute-start.10 = (bf16[4,128,256]{2,1,0:T(8,128)(2,1)S(1)}, bf16[4,128,256]{2,1,0:T(8,128)(2,1)S(1)}, u32[]{:S(2)}, u32[]{:S(2)}) collective-permute-start(bf16[4,128,256]{2,1,0:T(8,128)(2,1)S(1)} %bitcast.112), channel_id=1, source_target_pairs={{0,2},{1,3},{2,0},{3,1},{4,6},{5,7},{6,4},{7,5},{8,10},{9,11},{10,... | collective-permute-start | bytes 786440 | tf_op jit(solution)/shard_map/ppermute | solution.py:278
  74.0 6.0 %collective-permute-done.10 = bf16[4,128,256]{2,1,0:T(8,128)(2,1)S(1)} collective-permute-done((bf16[4,128,256]{2,1,0:T(8,128)(2,1)S(1)}, bf16[4,128,256]{2,1,0:T(8,128)(2,1)S(1)}, u32[]{:S(2)}, u32[]{:S(2)}) %collective-permute-start.10) | collective-permute-done | bytes 262176 | tf_op jit(solution)/shard_map/ppermute | solution.py:278
  80.3 8.2 %filters.3.filters_ref = bf16[256,8192]{1,0:T(8,128)(2,1)} custom-call(f32[64,128]{1,0:T(8,128)} %distance_ref.6, bf16[2,64,512]{2,1,0:T(8,128)(2,1)} %rbf_ref.3, bf16[2,512,256]{2,1,0:T(8,128)(2,1)} %filter_ref.3), custom_call_target="tpu_custom_call" | custom-call | flops 4294967296 | bytes 4194304 | tf_op jit(solution)/shard_map/filters/pallas_call | solution.py:72
  88.7 1.1 copy.50
  89.8 18.1 %update.3 = bf16[128,256]{1,0:T(8,128)(2,1)} custom-call(s32[1]{0:T(128)} %bitcast.brick_ref, bf16[2048,256]{1,0:T(8,128)(2,1)} %bitcast.101, bf16[2048,256]{1,0:T(8,128)(2,1)} %bitcast.102, bf16[2048,256]{1,0:T(8,128)(2,1)} %bitcast.103, bf16[2048,256]{1,0:T(8,128)(2,1)} %bitcast.104, f32[64,128]{1,0:T(8,128)} %distance_ref.6, s32[64,128]{1,0:T(8,128)} %neighbour_ref.3, ...), custom_call_target="tpu_custom_call" | custom-call | tf_op jit(solution)/shard_map/update/pallas_call | solution.py:236
  (51 shorter events, 1.9 us)
Async XLA Ops:
  0.0 14.1 %collective-permute-start.4 = (f32[1,3,128]{2,1,0:T(4,128)}, f32[1,3,128]{2,1,0:T(4,128)S(1)}, u32[]{:S(2)}, u32[]{:S(2)}) collective-permute-start(f32[1,3,128]{2,1,0:T(4,128)} %bitcast.123), channel_id=1, source_target_pairs={{0,8},{1,9},{2,10},{3,11},{4,12},{5,13},{6,14},{7,15},{8,0},{9,1},... | collective-permute-start | bytes 4616 | tf_op jit(solution)/shard_map/ppermute | solution.py:278
  4.1 12.1 %collective-permute-start = (bf16[1,128,256]{2,1,0:T(8,128)(2,1)}, bf16[1,128,256]{2,1,0:T(8,128)(2,1)S(1)}, u32[]{:S(2)}, u32[]{:S(2)}) collective-permute-start(bf16[1,128,256]{2,1,0:T(8,128)(2,1)} %bitcast.116), channel_id=1, source_target_pairs={{0,8},{1,9},{2,10},{3,11},{4,12},{5,13},{6,14},{7,15},{8,0},{9,1},... | collective-permute-start | bytes 196616 | tf_op jit(solution)/shard_map/ppermute | solution.py:278
  5.9 8.3 %copy-start.1 = (f32[3,128]{1,0:T(4,128)S(1)}, f32[3,128]{1,0:T(4,128)}, u32[]{:S(2)}) copy-start(f32[3,128]{1,0:T(4,128)} %param.13) | copy-start | bytes 4612
  5.9 10.3 %copy-start = (bf16[128,256]{1,0:T(8,128)(2,1)S(1)}, bf16[128,256]{1,0:T(8,128)(2,1)}, u32[]{:S(2)}) copy-start(bf16[128,256]{1,0:T(8,128)(2,1)} %param.12) | copy-start | bytes 196612
  14.1 13.8 %copy-start.2 = (f32[88,16]{0,1:T(8,128)S(1)}, f32[88,16]{0,1:T(8,128)}, u32[]{:S(2)}) copy-start(f32[88,16]{0,1:T(8,128)} %constant.119) | copy-start | bytes 16900
  14.2 3.7 %collective-permute-start.5 = (f32[2,3,128]{2,1,0:T(4,128)S(1)}, f32[2,3,128]{2,1,0:T(4,128)S(1)}, u32[]{:S(2)}, u32[]{:S(2)}) collective-permute-start(f32[2,3,128]{2,1,0:T(4,128)S(1)} %maximum_bitcast_fusion.2), channel_id=1, source_target_pairs={{0,4},{1,5},{2,6},{3,7},{4,0},{5,1},{6,2},{7,3},{8,12},{9,13},{10,... | collective-permute-start | bytes 9224 | tf_op jit(solution)/shard_map/ppermute | solution.py:278
  16.2 5.0 %collective-permute-start.1 = (bf16[2,128,256]{2,1,0:T(8,128)(2,1)S(1)}, bf16[2,128,256]{2,1,0:T(8,128)(2,1)S(1)}, u32[]{:S(2)}, u32[]{:S(2)}) collective-permute-start(bf16[2,128,256]{2,1,0:T(8,128)(2,1)S(1)} %maximum_bitcast_fusion), channel_id=1, source_target_pairs={{0,4},{1,5},{2,6},{3,7},{4,0},{5,1},{6,2},{7,3},{8,12},{9,13},{10,... | collective-permute-start | bytes 393224 | tf_op jit(solution)/shard_map/ppermute | solution.py:278
  17.9 5.0 %collective-permute-start.6 = (f32[4,3,128]{2,0,1:T(4,128)S(1)}, f32[4,3,128]{2,0,1:T(4,128)S(1)}, u32[]{:S(2)}, u32[]{:S(2)}) collective-permute-start(f32[4,3,128]{2,0,1:T(4,128)S(1)} %bitcast.119), channel_id=1, source_target_pairs={{0,2},{1,3},{2,0},{3,1},{4,6},{5,7},{6,4},{7,5},{8,10},{9,11},{10,... | collective-permute-start | bytes 18440 | tf_op jit(solution)/shard_map/ppermute | solution.py:278
  21.3 6.4 %collective-permute-start.2 = (bf16[4,128,256]{2,1,0:T(8,128)(2,1)S(1)}, bf16[4,128,256]{2,1,0:T(8,128)(2,1)S(1)}, u32[]{:S(2)}, u32[]{:S(2)}) collective-permute-start(bf16[4,128,256]{2,1,0:T(8,128)(2,1)S(1)} %bitcast.111), channel_id=1, source_target_pairs={{0,2},{1,3},{2,0},{3,1},{4,6},{5,7},{6,4},{7,5},{8,10},{9,11},{10,... | collective-permute-start | bytes 786440 | tf_op jit(solution)/shard_map/ppermute | solution.py:278
  22.9 7.3 %collective-permute-start.7 = (f32[8,3,128]{2,0,1:T(8,128)S(1)}, f32[8,3,128]{2,0,1:T(8,128)S(1)}, u32[]{:S(2)}, u32[]{:S(2)}) collective-permute-start(f32[8,3,128]{2,0,1:T(8,128)S(1)} %bitcast.117), channel_id=1, source_target_pairs={{0,1},{1,0},{2,3},{3,2},{4,5},{5,4},{6,7},{7,6},{8,9},{9,8},{10,11... | collective-permute-start | bytes 36872 | tf_op jit(solution)/shard_map/ppermute | solution.py:278
  27.9 12.4 %collective-permute-start.3 = (bf16[8,128,256]{2,1,0:T(8,128)(2,1)S(1)}, bf16[8,128,256]{2,1,0:T(8,128)(2,1)S(1)}, u32[]{:S(2)}, u32[]{:S(2)}) collective-permute-start(bf16[8,128,256]{2,1,0:T(8,128)(2,1)S(1)} %bitcast.109), channel_id=1, source_target_pairs={{0,1},{1,0},{2,3},{3,2},{4,5},{5,4},{6,7},{7,6},{8,9},{9,8},{10,11... | collective-permute-start | bytes 1572872 | tf_op jit(solution)/shard_map/ppermute | solution.py:278
  59.7 6.4 %collective-permute-start.8 = (bf16[1,128,256]{2,1,0:T(8,128)(2,1)}, bf16[1,128,256]{2,1,0:T(8,128)(2,1)S(1)}, u32[]{:S(2)}, u32[]{:S(2)}) collective-permute-start(bf16[1,128,256]{2,1,0:T(8,128)(2,1)} %bitcast.113), channel_id=1, source_target_pairs={{0,8},{1,9},{2,10},{3,11},{4,12},{5,13},{6,14},{7,15},{8,0},{9,1},... | collective-permute-start | bytes 196616 | tf_op jit(solution)/shard_map/ppermute | solution.py:278
  66.9 5.5 %collective-permute-start.9 = (bf16[2,128,256]{2,1,0:T(8,128)(2,1)S(1)}, bf16[2,128,256]{2,1,0:T(8,128)(2,1)S(1)}, u32[]{:S(2)}, u32[]{:S(2)}) collective-permute-start(bf16[2,128,256]{2,1,0:T(8,128)(2,1)S(1)} %maximum_bitcast_fusion.1), channel_id=1, source_target_pairs={{0,4},{1,5},{2,6},{3,7},{4,0},{5,1},{6,2},{7,3},{8,12},{9,13},{10,... | collective-permute-start | bytes 393224 | tf_op jit(solution)/shard_map/ppermute | solution.py:278
  72.6 7.5 %collective-permute-start.10 = (bf16[4,128,256]{2,1,0:T(8,128)(2,1)S(1)}, bf16[4,128,256]{2,1,0:T(8,128)(2,1)S(1)}, u32[]{:S(2)}, u32[]{:S(2)}) collective-permute-start(bf16[4,128,256]{2,1,0:T(8,128)(2,1)S(1)} %bitcast.112), channel_id=1, source_target_pairs={{0,2},{1,3},{2,0},{3,1},{4,6},{5,7},{6,4},{7,5},{8,10},{9,11},{10,... | collective-permute-start | bytes 786440 | tf_op jit(solution)/shard_map/ppermute | solution.py:278
  80.2 8.3 %collective-permute-start.11 = (bf16[8,128,256]{2,1,0:T(8,128)(2,1)S(1)}, bf16[8,128,256]{2,1,0:T(8,128)(2,1)S(1)}, u32[]{:S(2)}, u32[]{:S(2)}) collective-permute-start(bf16[8,128,256]{2,1,0:T(8,128)(2,1)S(1)} %bitcast.110), channel_id=1, source_target_pairs={{0,1},{1,0},{2,3},{3,2},{4,5},{5,4},{6,7},{7,6},{8,9},{9,8},{10,11... | collective-permute-start | bytes 1572872 | tf_op jit(solution)/shard_map/ppermute | solution.py:278
where the time goes:
time: 108 us
  Pallas kernels  62 us (57%)
  waiting for transfers between devices  23.4 us (22%)
  starting transfers between devices  13.6 us (13%)
  local copies, waits for them, and re-layouts  4.92 us (5%)
  other arithmetic  3.43 us (3%)
    pallas_call x2, Pallas kernels, layer_update(): pl.pallas_call(functools.partial(layer_kernel, field_scale), out_shape=ja...  36.2 us
    ppermute x12, waiting for transfers between devices, doubling_gather(): lax.ppermute(held, 'atom', [(i, i ^ distance) for i in range(bricks)])  23.4 us
    pallas_call x2, Pallas kernels, edge_filters(): pl.pallas_call(functools.partial(filter_kernel, layer), out_shape=jax.Sha...  16.5 us
    ppermute x12, starting transfers between devices, doubling_gather(): lax.ppermute(held, 'atom', [(i, i ^ distance) for i in range(bricks)])  13.6 us
    pallas_call x1, Pallas kernels, waves(): pl.pallas_call(wave_kernel, out_shape=jax.ShapeDtypeStruct((rows, atoms),...  9.36 us
    another operation x9, local copies, waits for them, and re-layouts, doubling_gather(): jnp.stack([jnp.where(low, held, other), jnp.where(low, other, held)], axi...  2.26 us
  transfers between devices with their start and end apart: 12, of which 6 were waited for; matrix products, arithmetic and copies ran while one was open for 5% of the time, Pallas kernels for 24%

commit v1 on v0

v1 whole, which is shorter than its diff:
```python
import functools
import math

import jax
import jax.numpy as jnp
import numpy as np
from jax import lax
from jax.experimental import pallas as pl
from jax.experimental.pallas import tpu as pltpu
from jax.sharding import PartitionSpec as P

MOST = 6
PAIRS = 88
SIDE = 2 * MOST + 1
GROUP = 8
MESH = pl.DeviceIdType.MESH


def fitted(function, terms):
    at = np.cos(np.pi * (np.arange(400) + 0.5) / 400) * 0.125 + 0.125
    values = function(np.sqrt(at))
    series = np.polynomial.chebyshev.Chebyshev.fit(at, values, terms - 1, domain=[0.0, 0.25])
    return [float(c) for c in series.convert(kind=np.polynomial.Polynomial).coef]


COS = fitted(lambda r: np.cos(2 * np.pi * r), 9)
SIN = fitted(lambda r: np.sin(2 * np.pi * r) / r, 8)


def horner(coefficients, x):
    total = jnp.full_like(x, coefficients[-1])
    for c in coefficients[-2::-1]:
        total = total * x + c
    return total


def cos_sin(turn):
    r = turn - jnp.floor(turn + 0.5)
    square = r * r
    return horner(COS, square), horner(SIN, square) * r


def pair_orders(shape):
    p = lax.broadcasted_iota(jnp.int32, shape, 0).astype(jnp.float32)
    row = jnp.floor((p - (MOST + 0.5)) * (1.0 / SIDE))
    m0 = row + 1.0
    m1 = jnp.where(m0 > 0.5, p - (MOST + 1) - row * SIDE - MOST, p)
    return m0, m1


def wave_weights(wave, scale):
    m0, m1, m2 = wave[0:1, :], wave[1:2, :], wave[2:3, :]
    flip = (m0 < 0) | ((m0 == 0) & (m1 < 0))
    m0, m1, m2 = (jnp.where(flip, -m, m) for m in (m0, m1, m2))
    pair = jnp.where(m0 == 0, m1, (MOST + 1) + (m0 - 1) * SIDE + m1 + MOST)
    many = wave.shape[1]
    one_pair = pair == lax.broadcasted_iota(jnp.int32, (PAIRS, many), 0)
    one_z = (m2 + 8) == lax.broadcasted_iota(jnp.int32, (16, many), 0)
    count = lax.dot_general(
        jnp.where(one_pair, 1.0, 0.0).astype(jnp.bfloat16),
        jnp.where(one_z, 1.0, 0.0).astype(jnp.bfloat16),
        (((1,), (1,)), ((), ())),
        preferred_element_type=jnp.float32,
    )
    n0, n1 = pair_orders((PAIRS, 16))
    n2 = lax.broadcasted_iota(jnp.int32, (PAIRS, 16), 1).astype(jnp.float32) - 8.0
    return count * scale / (1.0 + (n0 * n0 + n1 * n1 + n2 * n2) / 16.0)


def wave_rows(fraction, weight):
    width = fraction.shape[1]
    m0, m1 = pair_orders((PAIRS, width))
    cp, sp = cos_sin(m0 * fraction[0:1, :] + m1 * fraction[1:2, :])
    m2 = lax.broadcasted_iota(jnp.int32, (8, width), 0).astype(jnp.float32)
    cz, sz = cos_sin(m2 * fraction[2:3, :])

    def block(m, rows):
        if weight is not None:
            rows = [w * r for w, r in zip(m, rows)]
        return jnp.concatenate(rows, axis=0).astype(jnp.bfloat16)

    def factor(m):
        return None if weight is None else weight[:, 8 + m : 9 + m]

    yield 0, block((factor(0),) * 2, [cp, sp])
    for m in range(1, MOST + 1):
        c, s = cz[m : m + 1, :], sz[m : m + 1, :]
        a, b, g, h = cp * c, sp * s, sp * c, cp * s
        up, down = factor(m), factor(-m)
        yield 2 * PAIRS * (2 * m - 1), block((up, up, down, down), [a - b, g + h, a + b, g - h])


def step_kernel(
    grid, scale,
    features, fractional, distances, neighbours, edge_mask, wave_index,
    w_rbf, w_filter, w_mixing, w_short, w_long,
    out_ref,
    dist_v, neigh_v, mask_v, wave_v, rbf_v, filter_v, mixing_v, short_v, long_v,
    rbf_t, filter_t, both, weight_v, near16, edge_v,
    source_x, target_x, source_rows, target_rows, matrix,
    states, beside, table, filters, partial, own_part, arrived, message,
    in_sem, near_send, near_recv, col_send, col_recv, row_send, row_recv,
    place_send, place_recv,
):
    across, along = grid
    bricks = across * along
    layers = w_rbf.shape[0]
    slots, rows = distances.shape
    count, hidden = w_rbf.shape[1:]
    width = w_filter.shape[2]
    me = lax.axis_index("atom")
    a, b = me // along, lax.rem(me, along)
    after = lax.rem(me + 1, bricks)
    before = lax.rem(me + bricks - 1, bricks)

    def column(k):
        return lax.rem(a + k, across) * along + b

    def line(k):
        return a * along + lax.rem(b + k, along)

    def to(index):
        return {"atom": index}

    peers = [column(k) for k in range(1, across)] + [line(k) for k in range(1, along)]
    peers += [before, after]
    barrier = pltpu.get_barrier_semaphore()
    for peer in peers:
        pl.semaphore_signal(barrier, inc=1, device_id=to(peer), device_id_type=MESH)

    loads = [
        (distances, dist_v), (w_rbf, rbf_v), (w_filter, filter_v), (wave_index, wave_v),
        (features, states.at[0, 0]), (fractional, source_x.at[0]), (fractional, target_x.at[0]),
        (neighbours, neigh_v), (edge_mask, mask_v), (w_mixing, mixing_v), (w_long, long_v),
        (w_short, short_v),
    ]
    loads = [pltpu.make_async_copy(x, y, in_sem.at[i]) for i, (x, y) in enumerate(loads)]
    for load in loads:
        load.start()
    pl.semaphore_wait(barrier, len(peers))

    def remote(source, target, send, recv, index):
        return pltpu.make_async_remote_copy(
            src_ref=source, dst_ref=target, send_sem=send, recv_sem=recv,
            device_id=to(index), device_id_type=MESH,
        )

    def send_states(layer, source):
        near = [
            remote(source, beside.at[layer, 0], near_send.at[layer, 0], near_recv.at[layer, 0], after),
            remote(source, beside.at[layer, 1], near_send.at[layer, 1], near_recv.at[layer, 1], before),
        ]
        far = [
            remote(
                source, states.at[layer, k], col_send.at[layer, k], col_recv.at[layer, k], column(k)
            )
            for k in range(1, across)
        ]
        for copy in near + far:
            copy.start()
        return near, far

    placed = [
        remote(fractional, source_x.at[k], place_send.at[0, k], place_recv.at[0, k], column(k))
        for k in range(1, across)
    ] + [
        remote(fractional, target_x.at[k], place_send.at[1, k], place_recv.at[1, k], line(k))
        for k in range(1, along)
    ]
    for copy in placed:
        copy.start()
    near, far = send_states(0, features)

    def transposed(x):
        return x.astype(jnp.float32).T.astype(jnp.bfloat16)

    center = 0.5 + 4.5 * lax.broadcasted_iota(jnp.int32, (count, rows), 0).astype(jnp.float32) / (
        count - 1
    )

    def edge_filters(layer):
        rbf_t[...] = transposed(rbf_v[layer].astype(jnp.float32) * 0.5)
        filter_t[...] = transposed(filter_v[layer])
        for first in range(0, slots, GROUP):
            parts = []
            for slot in range(first, first + GROUP):
                offset = dist_v[slot : slot + 1, :] - center
                parts.append(jnp.exp(-4.0 * offset * offset).astype(jnp.bfloat16))
            half = jnp.dot(
                rbf_t[...], jnp.concatenate(parts, axis=1), preferred_element_type=jnp.float32
            )
            inner = (half + half * jnp.tanh(half)).astype(jnp.bfloat16)
            filters[:, first * rows : (first + GROUP) * rows] = jnp.dot(
                filter_t[...], inner, preferred_element_type=jnp.float32
            ).astype(jnp.bfloat16)

    place = lax.broadcasted_iota(jnp.int32, (3 * rows, rows), 0).astype(jnp.int16)

    def gather(first, last):
        total = message[...]
        for begin in range(first, last, GROUP):
            picks = []
            for slot in range(begin, begin + GROUP):
                hit = place == near16[slot : slot + 1, :]
                picks.append(jnp.where(hit, jnp.bfloat16(1), jnp.bfloat16(0)))
            gathered = jnp.dot(
                table[...], jnp.concatenate(picks, axis=1), preferred_element_type=jnp.float32
            )
            for at in range(GROUP):
                slot = begin + at
                factor = filters[:, slot * rows : (slot + 1) * rows].astype(jnp.float32)
                factor = factor * edge_v[slot : slot + 1, :]
                total = total + gathered[:, at * rows : (at + 1) * rows] * factor
        message[...] = total

    def send_partial(layer):
        held = [states[layer, k] for k in range(across)]
        product = jnp.dot(
            matrix[...], jnp.concatenate(held, axis=0), preferred_element_type=jnp.float32
        )
        copies = []
        for k in range(1, along):
            partial[layer, k] = product[k * rows : (k + 1) * rows, :].astype(jnp.bfloat16)
            copies.append(
                remote(
                    partial.at[layer, k], arrived.at[layer, k], row_send.at[layer, k],
                    row_recv.at[layer, k], line(k),
                )
            )
            copies[-1].start()
        own_part[...] = product[0:rows, :]
        return copies

    def update(layer):
        field = own_part[...]
        for k in range(1, along):
            field = field + arrived[layer, k].astype(jnp.float32)
        short = jnp.dot(
            message[...].T.astype(jnp.bfloat16), short_v[layer], preferred_element_type=jnp.float32
        )
        step = short + jnp.dot(
            field.astype(jnp.bfloat16), both[layer], preferred_element_type=jnp.float32
        )
        state = states[layer, 0].astype(jnp.float32) + step * jax.nn.sigmoid(step)
        return state.astype(jnp.bfloat16)

    for load in loads[:4]:
        load.wait()
    edge_filters(0)

    for load in loads[4:]:
        load.wait()
    for copy in placed:
        copy.wait_recv()
    weight_v[...] = wave_weights(wave_v[...], scale)
    weight = weight_v[...]

    def sources(k, carry):
        for row, block in wave_rows(source_x[k], None):
            source_rows[row : row + block.shape[0], pl.ds(pl.multiple_of(k * rows, rows), rows)] = block
        return carry

    def targets(k, carry):
        at = lax.rem(along - k, along)
        for row, block in wave_rows(target_x[at], weight):
            target_rows[row : row + block.shape[0], pl.ds(pl.multiple_of(k * rows, rows), rows)] = block
        return carry

    lax.fori_loop(0, across, sources, 0)
    lax.fori_loop(0, along, targets, 0)
    matrix[...] = lax.dot_general(
        target_rows[...], source_rows[...], (((0,), (0,)), ((), ())),
        preferred_element_type=jnp.float32,
    ).astype(jnp.bfloat16)
    for layer in range(layers):
        both[layer] = jnp.dot(
            mixing_v[layer], long_v[layer], preferred_element_type=jnp.float32
        ).astype(jnp.bfloat16)
    near16[...] = neigh_v[...].astype(jnp.int16)
    envelope = 0.5 * (cos_sin(dist_v[...] * 0.1)[0] + 1.0)
    edge_v[...] = envelope * mask_v[...].astype(jnp.float32)

    sent = list(placed)
    for layer in range(layers):
        if layer > 0:
            edge_filters(layer)
        message[...] = jnp.zeros_like(message)
        for copy in near:
            copy.wait_recv()
        table[:, 0:rows] = transposed(beside[layer, 0])
        table[:, rows : 2 * rows] = transposed(states[layer, 0])
        table[:, 2 * rows : 3 * rows] = transposed(beside[layer, 1])
        if layer > 0:
            gather(0, slots // 2)
        for copy in far:
            copy.wait_recv()
        copies = send_partial(layer)
        gather(slots // 2 if layer > 0 else 0, slots)
        for copy in copies:
            copy.wait_recv()
        sent += near + far + copies
        state = update(layer)
        if layer + 1 < layers:
            states[layer + 1, 0] = state
            near, far = send_states(layer + 1, states.at[layer + 1, 0])
        else:
            out_ref[...] = state
    for copy in sent:
        copy.wait_send()


def per_device(
    features, fractional, distances, neighbours, edge_mask, wave_index,
    w_rbf, w_filter, w_mixing, w_short, w_long,
):
    bricks = lax.axis_size("atom")
    along = max(n for n in range(1, bricks + 1) if bricks % n == 0 and n * n <= bricks)
    across = bricks // along
    rows, width = features.shape
    slots = distances.shape[0]
    layers, count, hidden = w_rbf.shape
    scale = 4.0 / math.sqrt(wave_index.shape[1]) / math.sqrt(rows * bricks)
    waves = 2 * PAIRS * SIDE
    half, full = jnp.bfloat16, jnp.float32
    dma = pltpu.SemaphoreType.DMA
    V = pltpu.VMEM
    scratch = [
        V(distances.shape, full), V(neighbours.shape, jnp.int32), V(edge_mask.shape, jnp.int32),
        V(wave_index.shape, jnp.int32), V(w_rbf.shape, half), V(w_filter.shape, half),
        V(w_mixing.shape, half), V(w_short.shape, half), V(w_long.shape, half),
        V((hidden, count), half), V((width, hidden), half), V((layers, width, width), half),
        V((PAIRS, 16), full), V((slots, rows), jnp.int16), V((slots, rows), full),
        V((across,) + fractional.shape, full), V((along,) + fractional.shape, full),
        V((waves, across * rows), half), V((waves, along * rows), half),
        V((along * rows, across * rows), half),
        V((layers, across, rows, width), half), V((layers, 2, rows, width), half),
        V((width, 3 * rows), half), V((width, slots * rows), half),
        V((layers, along, rows, width), half), V((rows, width), full),
        V((layers, along, rows, width), half), V((width, rows), full),
        dma((12,)), dma((layers, 2)), dma((layers, 2)),
        dma((layers, across)), dma((layers, across)), dma((layers, along)), dma((layers, along)),
        dma((2, max(across, along))), dma((2, max(across, along))),
    ]
    return pl.pallas_call(
        functools.partial(step_kernel, (across, along), scale),
        out_shape=jax.ShapeDtypeStruct(features.shape, features.dtype),
        in_specs=[pl.BlockSpec(memory_space=pl.ANY)] * 11,
        out_specs=pl.BlockSpec(memory_space=pltpu.VMEM),
        scratch_shapes=scratch,
        compiler_params=pltpu.CompilerParams(
            collective_id=0, has_side_effects=True, vmem_limit_bytes=60 << 20
        ),
        name="step",
    )(
        features, fractional, distances, neighbours, edge_mask, wave_index,
        w_rbf, w_filter, w_mixing, w_short, w_long,
    )


def solution(mesh):
    split_rows = P(("rep", "atom"), None)
    split_columns = P(None, ("rep", "atom"))
    in_specs = (split_rows,) + (split_columns,) * 4 + (P(),) * 6
    return jax.shard_map(
        per_device, mesh=mesh, in_specs=in_specs, out_specs=split_rows, check_vma=False
    )
```

time: 108 us -> 33.3 us (0.31)
  Pallas kernels: 62 us -> 31.4 us
  waiting for transfers between devices: 23.4 us -> 0 us
  starting transfers between devices: 13.6 us -> 0 us
  local copies, waits for them, and re-layouts: 4.92 us -> 1.47 us
  other arithmetic: 3.43 us -> 0 us
    pallas_call x5 -> x1, Pallas kernels: 62 us -> 31.4 us  [per_device(): pl.pallas_call(functools.partial(step_kernel, (across, along), scale), ou...]
    ppermute x12 -> x0, waiting for transfers between devices: 23.4 us -> none  [doubling_gather(): lax.ppermute(held, 'atom', [(i, i ^ distance) for i in range(bricks)])]
    ppermute x12 -> x0, starting transfers between devices: 13.6 us -> none  [doubling_gather(): lax.ppermute(held, 'atom', [(i, i ^ distance) for i in range(bricks)])]
    another operation x9 -> x0, local copies, waits for them, and re-layouts: 2.26 us -> none  [doubling_gather(): jnp.stack([jnp.where(low, held, other), jnp.where(low, other, held)], axi...]
    reshape x1 -> x0, local copies, waits for them, and re-layouts: 1.9 us -> none  [row_weights(): jnp.broadcast_to(weight[:, None, :], (len(PAIRS), 2, Z_ROWS)).reshape(-1, 1)]
    another operation x21 -> x0, other arithmetic: 1.63 us -> none  [doubling_gather(): jnp.stack([jnp.where(low, held, other), jnp.where(low, other, held)], axi...]
  transfers between devices with their start and end apart: 12 -> 0, of which waited for: 6 -> 0; matrix products, arithmetic and copies ran while one was open for 5% -> 0% of each run, Pallas kernels for 24% -> 0%
where the time goes in v1:
time: 33.3 us; the launch traced here: 32.9 us
  Pallas kernels  31.4 us (94%)
  local copies, waits for them, and re-layouts  1.47 us (4%)
    pallas_call x1, Pallas kernels, per_device(): pl.pallas_call(functools.partial(step_kernel, (across, along), scale), ou...  31.4 us
    unnamed x1, local copies, waits for them, and re-layouts  1.47 us

profile of v1, /device:TPU:0, one launch (start us, length us, event | category | flops | bytes accessed | tf_op | source)
XLA Modules:
  0.0 32.9 jit_solution(17856790510033515432)
XLA Ops:
  0.0 31.4 %step.1 = bf16[128,256]{1,0:T(8,128)(2,1)} custom-call(bf16[128,256]{1,0:T(8,128)(2,1)} %features.1, f32[3,128]{1,0:T(4,128)} %fractional.1, f32[64,128]{1,0:T(8,128)} %distances.1, s32[64,128]{1,0:T(8,128)} %neighbours.1, s32[64,128]{1,0:T(8,128)} %edge_mask.1, s32[3,2048]{1,0:T(4,128)} %wave_index.1, bf16[2,64,512]{2,1,0:T(8,128)(2,1)} %w_rbf.1, ...), custom_call_target="tpu_custom_call" | custom-call | tf_op jit(solution)/shard_map/step/pallas_call | solution.py:344
  31.4 1.5 %copy.13 = bf16[128,256]{1,0:T(8,128)(2,1)} copy(bf16[128,256]{1,0:T(8,128)(2,1)} %step.1) | data formatting | bytes 131072

commit v2 on v1

v2 whole, which is shorter than its diff:
```python
import functools
import math

import jax
import jax.numpy as jnp
import numpy as np
from jax import lax
from jax.experimental import pallas as pl
from jax.experimental.pallas import tpu as pltpu
from jax.sharding import PartitionSpec as P

MOST = 6
PAIRS = 88
SIDE = 2 * MOST + 1
GROUP = 8
EARLY, MIDDLE, PRE, SECOND, LATER = 1, 3, 7, 2, 0
MESH = pl.DeviceIdType.MESH


def fitted(function, terms):
    at = np.cos(np.pi * (np.arange(400) + 0.5) / 400) * 0.125 + 0.125
    values = function(np.sqrt(at))
    series = np.polynomial.chebyshev.Chebyshev.fit(at, values, terms - 1, domain=[0.0, 0.25])
    return [float(c) for c in series.convert(kind=np.polynomial.Polynomial).coef]


COS = fitted(lambda r: np.cos(2 * np.pi * r), 9)
SIN = fitted(lambda r: np.sin(2 * np.pi * r) / r, 8)


def horner(coefficients, x):
    total = jnp.full_like(x, coefficients[-1])
    for c in coefficients[-2::-1]:
        total = total * x + c
    return total


def cos_sin(turn):
    r = turn - jnp.floor(turn + 0.5)
    square = r * r
    return horner(COS, square), horner(SIN, square) * r


def pair_orders(shape):
    p = lax.broadcasted_iota(jnp.int32, shape, 0).astype(jnp.float32)
    row = jnp.floor((p - (MOST + 0.5)) * (1.0 / SIDE))
    m0 = row + 1.0
    m1 = jnp.where(m0 > 0.5, p - (MOST + 1) - row * SIDE - MOST, p)
    return m0, m1


def wave_weights(wave, scale):
    m0, m1, m2 = wave[0:1, :], wave[1:2, :], wave[2:3, :]
    flip = (m0 < 0) | ((m0 == 0) & (m1 < 0))
    m0, m1, m2 = (jnp.where(flip, -m, m) for m in (m0, m1, m2))
    pair = jnp.where(m0 == 0, m1, (MOST + 1) + (m0 - 1) * SIDE + m1 + MOST)
    many = wave.shape[1]
    one_pair = pair == lax.broadcasted_iota(jnp.int32, (PAIRS, many), 0)
    one_z = (m2 + 8) == lax.broadcasted_iota(jnp.int32, (16, many), 0)
    count = lax.dot_general(
        jnp.where(one_pair, 1.0, 0.0).astype(jnp.bfloat16),
        jnp.where(one_z, 1.0, 0.0).astype(jnp.bfloat16),
        (((1,), (1,)), ((), ())),
        preferred_element_type=jnp.float32,
    )
    n0, n1 = pair_orders((PAIRS, 16))
    n2 = lax.broadcasted_iota(jnp.int32, (PAIRS, 16), 1).astype(jnp.float32) - 8.0
    return count * scale / (1.0 + (n0 * n0 + n1 * n1 + n2 * n2) / 16.0)


def wave_rows(fraction, orders, weights):
    width = fraction.shape[1]
    cp, sp = cos_sin(orders[0] * fraction[0:1, :] + orders[1] * fraction[1:2, :])
    m2 = lax.broadcasted_iota(jnp.int32, (8, width), 0).astype(jnp.float32)
    cz, sz = cos_sin(m2 * fraction[2:3, :])
    for m in range(MOST + 1):
        if m == 0:
            signs, terms = (0, 0), (cp, sp)
        else:
            c, s = cz[m : m + 1, :], sz[m : m + 1, :]
            x, y, u, v = cp * c, sp * s, sp * c, cp * s
            signs, terms = (m, m, -m, -m), (x - y, u + v, x + y, u - v)
        row = 2 * PAIRS * max(2 * m - 1, 0)
        forms = [terms]
        if weights is not None:
            forms.append([weights[MOST + at] * term for at, term in zip(signs, terms)])
        yield row, [jnp.concatenate(form, axis=0).astype(jnp.bfloat16) for form in forms]


def step_kernel(
    grid, scale,
    features, fractional, distances, neighbours, edge_mask, wave_index,
    w_rbf, w_filter, w_mixing, w_short, w_long,
    out_ref,
    dist_v, neigh_v, mask_v, wave_v, rbf_v, filter_v, mixing_v, short_v, long_v,
    rbf_t, filter_t, both, orders, weights, near16, edge_v,
    source_x, target_x, source_rows, target_rows, target_t, matrix, flipped,
    own, beside, line_held, plane_held, table, filters,
    plane_part, line_part, plane_got, line_got, own_field, message,
    in_sem, near_send, near_recv, line_send, line_recv, plane_send, plane_recv,
    place_send, place_recv,
):
    across, along = grid
    bricks = across * along
    layers = w_rbf.shape[0]
    slots, rows = distances.shape
    count, hidden = w_rbf.shape[1:]
    width = w_filter.shape[2]
    half = width // 2
    me = lax.axis_index("atom")
    a, b = me // along, lax.rem(me, along)
    after = lax.rem(me + 1, bricks)
    before = lax.rem(me + bricks - 1, bricks)

    def line(k):
        return lax.rem(a + k, across) * along + b

    def plane(k):
        return a * along + lax.rem(b + k, along)

    def to(index):
        return {"atom": index}

    peers = [line(k) for k in range(1, across)] + [plane(k) for k in range(1, along)]
    peers += [before, after]
    barrier = pltpu.get_barrier_semaphore()
    for peer in peers:
        pl.semaphore_signal(barrier, inc=1, device_id=to(peer), device_id_type=MESH)

    loads = [
        (distances, dist_v), (w_rbf, rbf_v), (w_filter, filter_v),
        (features.at[:, 0:half], own.at[0, 0]), (features.at[:, half:width], own.at[0, 1]),
        (fractional, source_x.at[0]), (fractional, target_x.at[0]), (wave_index, wave_v),
        (neighbours, neigh_v), (edge_mask, mask_v), (w_mixing, mixing_v), (w_long, long_v),
        (w_short, short_v),
    ]
    loads = [pltpu.make_async_copy(x, y, in_sem.at[i]) for i, (x, y) in enumerate(loads)]
    for load in loads:
        load.start()

    def remote(source, target, send, recv, index):
        return pltpu.make_async_remote_copy(
            src_ref=source, dst_ref=target, send_sem=send, recv_sem=recv,
            device_id=to(index), device_id_type=MESH,
        )

    def send_states(layer):
        far = [
            remote(
                own.at[layer, 0], line_held.at[layer, k], line_send.at[layer, 0, k],
                line_recv.at[layer, 0, k], line(k),
            )
            for k in range(1, across)
        ] + [
            remote(
                own.at[layer, 1], plane_held.at[layer, k], plane_send.at[layer, 0, k],
                plane_recv.at[layer, 0, k], plane(k),
            )
            for k in range(1, along)
        ]
        near, cross = [], []
        for at, index in enumerate((after, before)):
            for part in range(2):
                copy = remote(
                    own.at[layer, part], beside.at[layer, at, part], near_send.at[layer, at, part],
                    near_recv.at[layer, at, part], index,
                )
                (cross if part else near).append(copy)
        for copy in far:
            copy.start()
        return near, cross, far

    first, last = b == 0, b == along - 1
    sends, takes = (last, first), (first, last)

    def start_near(near, cross):
        for at in range(2):
            near[at].start()
            pl.when(sends[at])(cross[at].start)

    def wait_near(near, cross):
        for at in range(2):
            near[at].wait_recv()
            pl.when(takes[at])(cross[at].wait_recv)

    def end_near(near, cross):
        for at in range(2):
            near[at].wait_send()
            pl.when(sends[at])(cross[at].wait_send)

    def transposed(x):
        return x.astype(jnp.float32).T.astype(jnp.bfloat16)

    center = 0.5 + 4.5 * lax.broadcasted_iota(jnp.int32, (count, rows), 0).astype(jnp.float32) / (
        count - 1
    )
    blocks = slots // GROUP

    def edge_weights(layer):
        rbf_t[layer] = transposed(rbf_v[layer].astype(jnp.float32) * 0.5)
        filter_t[layer] = transposed(filter_v[layer])

    def edge_filters(layer, begin, end):
        for first in range(begin * GROUP, end * GROUP, GROUP):
            parts = []
            for slot in range(first, first + GROUP):
                offset = dist_v[slot : slot + 1, :] - center
                parts.append(jnp.exp(-4.0 * offset * offset).astype(jnp.bfloat16))
            hidden_half = jnp.dot(
                rbf_t[layer], jnp.concatenate(parts, axis=1), preferred_element_type=jnp.float32
            )
            inner = (hidden_half + hidden_half * jnp.tanh(hidden_half)).astype(jnp.bfloat16)
            filters[layer, :, first * rows : (first + GROUP) * rows] = jnp.dot(
                filter_t[layer], inner, preferred_element_type=jnp.float32
            ).astype(jnp.bfloat16)

    place = lax.broadcasted_iota(jnp.int32, (3 * rows, rows), 0).astype(jnp.int16)

    def gather(layer, begin, end):
        total = message[...]
        for first in range(begin * GROUP, end * GROUP, GROUP):
            picks = []
            for slot in range(first, first + GROUP):
                hit = place == near16[slot : slot + 1, :]
                picks.append(jnp.where(hit, jnp.bfloat16(1), jnp.bfloat16(0)))
            gathered = jnp.dot(
                table[...], jnp.concatenate(picks, axis=1), preferred_element_type=jnp.float32
            )
            for at in range(GROUP):
                slot = first + at
                factor = filters[layer, :, slot * rows : (slot + 1) * rows].astype(jnp.float32)
                factor = factor * edge_v[slot : slot + 1, :]
                total = total + gathered[:, at * rows : (at + 1) * rows] * factor
        message[...] = total

    def send_partial(layer):
        held = [own[layer, 0]] + [line_held[layer, k] for k in range(1, across)]
        down = jnp.dot(
            matrix[...], jnp.concatenate(held, axis=0), preferred_element_type=jnp.float32
        )
        held = [own[layer, 1]] + [plane_held[layer, along - k] for k in range(1, along)]
        up = jnp.dot(
            flipped[...], jnp.concatenate(held, axis=0), preferred_element_type=jnp.float32
        )
        copies = []
        for k in range(1, across):
            line_part[layer, k] = up[k * rows : (k + 1) * rows, :].astype(jnp.bfloat16)
            copies.append(
                remote(
                    line_part.at[layer, k], line_got.at[layer, k], line_send.at[layer, 1, k],
                    line_recv.at[layer, 1, k], line(across - k),
                )
            )
        for k in range(1, along):
            plane_part[layer, k] = down[k * rows : (k + 1) * rows, :].astype(jnp.bfloat16)
            copies.append(
                remote(
                    plane_part.at[layer, k], plane_got.at[layer, k], plane_send.at[layer, 1, k],
                    plane_recv.at[layer, 1, k], plane(k),
                )
            )
        for copy in copies:
            copy.start()
        own_field[0] = down[0:rows, :]
        own_field[1] = up[0:rows, :]
        return copies

    def update(layer):
        short = jnp.dot(
            message[...].T.astype(jnp.bfloat16), short_v[layer], preferred_element_type=jnp.float32
        )
        left, right = own_field[0], own_field[1]
        for k in range(1, along):
            left = left + plane_got[layer, k].astype(jnp.float32)
        for k in range(1, across):
            right = right + line_got[layer, k].astype(jnp.float32)
        field = jnp.concatenate([left, right], axis=1).astype(jnp.bfloat16)
        step = short + jnp.dot(field, both[layer], preferred_element_type=jnp.float32)
        state = jnp.concatenate([own[layer, 0], own[layer, 1]], axis=1).astype(jnp.float32)
        return (state + step * jax.nn.sigmoid(step)).astype(jnp.bfloat16)

    def fill_table(layer):
        def put(at, part, ref):
            table[part * half : (part + 1) * half, at * rows : (at + 1) * rows] = transposed(ref[...])

        put(0, 0, beside.at[layer, 0, 0])
        put(1, 0, own.at[layer, 0])
        put(1, 1, own.at[layer, 1])
        put(2, 0, beside.at[layer, 1, 0])
        for at, slot in ((0, 1 % along), (1, along - 1)):
            pl.when(takes[at])(functools.partial(put, 2 * at, 1, beside.at[layer, at, 1]))
            pl.when(jnp.logical_not(takes[at]))(
                functools.partial(put, 2 * at, 1, plane_held.at[layer, slot])
            )

    done = [0] * (layers + 1)

    def fill(layer, end):
        if layer < layers and done[layer] < end:
            if done[layer] == 0:
                edge_weights(layer)
            edge_filters(layer, done[layer], end)
            done[layer] = end

    for load in loads[:3]:
        load.wait()
    fill(0, EARLY)
    for load in loads[3:7]:
        load.wait()
    pl.semaphore_wait(barrier, len(peers))
    placed_plane = [
        remote(fractional, target_x.at[k], place_send.at[1, k], place_recv.at[1, k], plane(k))
        for k in range(1, along)
    ]
    placed_line = [
        remote(fractional, source_x.at[k], place_send.at[0, k], place_recv.at[0, k], line(k))
        for k in range(1, across)
    ]
    for copy in placed_line + placed_plane:
        copy.start()
    near, cross, far = send_states(0)
    for load in loads[7:]:
        load.wait()
    weight = wave_weights(wave_v[...], scale)
    for m in range(-MOST, MOST + 1):
        weights[MOST + m] = jnp.broadcast_to(weight[:, 8 + m : 9 + m], (PAIRS, rows))
    for at, order in enumerate(pair_orders((PAIRS, rows))):
        orders[at] = order
    for row, (plain, weighted) in wave_rows(source_x[0], orders, weights):
        source_rows[row : row + plain.shape[0], 0:rows] = plain
        target_rows[row : row + plain.shape[0], 0:rows] = weighted
    fill(0, MIDDLE)
    start_near(near, cross)
    for layer in range(layers):
        both[layer] = jnp.dot(
            mixing_v[layer], long_v[layer], preferred_element_type=jnp.float32
        ).astype(jnp.bfloat16)
    near16[...] = neigh_v[...].astype(jnp.int16)
    envelope = 0.5 * (cos_sin(dist_v[...] * 0.1)[0] + 1.0)
    edge_v[...] = envelope * mask_v[...].astype(jnp.float32)
    fill(0, PRE)

    def lanes(k):
        return pl.ds(pl.multiple_of(k * rows, rows), rows)

    def sources(k, carry):
        for row, (plain,) in wave_rows(source_x[k], orders, None):
            source_rows[row : row + plain.shape[0], lanes(k)] = plain
        return carry

    def targets(k, carry):
        for row, (_, weighted) in wave_rows(target_x[along - k], orders, weights):
            target_rows[row : row + weighted.shape[0], lanes(k)] = weighted
        return carry

    for copy in placed_plane:
        copy.wait_recv()
    lax.fori_loop(1, along, targets, 0)
    target_t[...] = target_rows[...].T
    for copy in placed_line:
        copy.wait_recv()
    lax.fori_loop(1, across, sources, 0)
    product = jnp.dot(target_t[...], source_rows[...], preferred_element_type=jnp.float32)
    matrix[...] = product.astype(jnp.bfloat16)
    flipped[...] = product.T.astype(jnp.bfloat16)

    sent = placed_line + placed_plane
    for layer in range(layers):
        message[...] = jnp.zeros_like(message)
        if layer > 0:
            fill(layer, min(done[layer] + LATER, blocks))
            start_near(near, cross)
            fill(layer, blocks)
        for copy in far:
            copy.wait_recv()
        copies = send_partial(layer)
        fill(layer, blocks)
        wait_near(near, cross)
        fill_table(layer)
        gather(layer, 0, blocks)
        fill(layer + 1, SECOND)
        for copy in copies:
            copy.wait_recv()
        sent += far + copies
        state = update(layer)
        end_near(near, cross)
        if layer + 1 < layers:
            own[layer + 1, 0] = state[:, 0:half]
            own[layer + 1, 1] = state[:, half:width]
            near, cross, far = send_states(layer + 1)
        else:
            out_ref[...] = state
    for copy in sent:
        copy.wait_send()


def per_device(
    features, fractional, distances, neighbours, edge_mask, wave_index,
    w_rbf, w_filter, w_mixing, w_short, w_long,
):
    bricks = lax.axis_size("atom")
    along = max(n for n in range(1, bricks + 1) if bricks % n == 0 and n * n <= bricks)
    across = bricks // along
    rows, width = features.shape
    slots = distances.shape[0]
    layers, count, hidden = w_rbf.shape
    scale = 4.0 / math.sqrt(wave_index.shape[1]) / math.sqrt(rows * bricks)
    waves = 2 * PAIRS * SIDE
    half, full = jnp.bfloat16, jnp.float32
    dma = pltpu.SemaphoreType.DMA
    V = pltpu.VMEM
    part = (rows, width // 2)
    scratch = [
        V(distances.shape, full), V(neighbours.shape, jnp.int32), V(edge_mask.shape, jnp.int32),
        V(wave_index.shape, jnp.int32), V(w_rbf.shape, half), V(w_filter.shape, half),
        V(w_mixing.shape, half), V(w_short.shape, half), V(w_long.shape, half),
        V((layers, hidden, count), half), V((layers, width, hidden), half),
        V((layers, width, width), half),
        V((2, PAIRS, rows), full), V((SIDE, PAIRS, rows), full), V((slots, rows), jnp.int16), V((slots, rows), full),
        V((across,) + fractional.shape, full), V((along,) + fractional.shape, full),
        V((waves, across * rows), half), V((waves, along * rows), half),
        V((along * rows, waves), half),
        V((along * rows, across * rows), half), V((across * rows, along * rows), half),
        V((layers, 2) + part, half), V((layers, 2, 2) + part, half),
        V((layers, across) + part, half), V((layers, along) + part, half),
        V((width, 3 * rows), half), V((layers, width, slots * rows), half),
        V((layers, along) + part, half), V((layers, across) + part, half),
        V((layers, along) + part, half), V((layers, across) + part, half),
        V((2,) + part, full), V((width, rows), full),
        dma((13,)), dma((layers, 2, 2)), dma((layers, 2, 2)),
        dma((layers, 2, across)), dma((layers, 2, across)),
        dma((layers, 2, along)), dma((layers, 2, along)),
        dma((2, max(across, along))), dma((2, max(across, along))),
    ]
    return pl.pallas_call(
        functools.partial(step_kernel, (across, along), scale),
        out_shape=jax.ShapeDtypeStruct(features.shape, features.dtype),
        in_specs=[pl.BlockSpec(memory_space=pl.ANY)] * 11,
        out_specs=pl.BlockSpec(memory_space=pltpu.VMEM),
        scratch_shapes=scratch,
        compiler_params=pltpu.CompilerParams(
            collective_id=0, has_side_effects=True, vmem_limit_bytes=60 << 20
        ),
        name="step",
    )(
        features, fractional, distances, neighbours, edge_mask, wave_index,
        w_rbf, w_filter, w_mixing, w_short, w_long,
    )


def solution(mesh):
    split_rows = P(("rep", "atom"), None)
    split_columns = P(None, ("rep", "atom"))
    in_specs = (split_rows,) + (split_columns,) * 4 + (P(),) * 6
    return jax.shard_map(
        per_device, mesh=mesh, in_specs=in_specs, out_specs=split_rows, check_vma=False
    )
```

time: 33.3 us -> 31.6 us (0.949)
  Pallas kernels: 31.4 us -> 29.9 us
    pallas_call x1, Pallas kernels: 31.4 us -> 29.9 us  [per_device(): pl.pallas_call(functools.partial(step_kernel, (across, along), scale), ou...]
where the time goes in v2:
time: 31.6 us; the launch traced here: 31.4 us
  Pallas kernels  29.9 us (95%)
  local copies, waits for them, and re-layouts  1.47 us (5%)
    pallas_call x1, Pallas kernels, per_device(): pl.pallas_call(functools.partial(step_kernel, (across, along), scale), ou...  29.9 us
    unnamed x1, local copies, waits for them, and re-layouts  1.47 us

profile of v2, /device:TPU:0, one launch (start us, length us, event | category | flops | bytes accessed | tf_op | source)
XLA Modules:
  0.0 31.4 jit_solution(16380149035730569821)
XLA Ops:
  0.0 29.9 %step.1 = bf16[128,256]{1,0:T(8,128)(2,1)} custom-call(bf16[128,256]{1,0:T(8,128)(2,1)} %features.1, f32[3,128]{1,0:T(4,128)} %fractional.1, f32[64,128]{1,0:T(8,128)} %distances.1, s32[64,128]{1,0:T(8,128)} %neighbours.1, s32[64,128]{1,0:T(8,128)} %edge_mask.1, s32[3,2048]{1,0:T(4,128)} %wave_index.1, bf16[2,64,512]{2,1,0:T(8,128)(2,1)} %w_rbf.1, ...), custom_call_target="tpu_custom_call" | custom-call | tf_op jit(solution)/shard_map/step/pallas_call | solution.py:435
  29.9 1.5 %copy.13 = bf16[128,256]{1,0:T(8,128)(2,1)} copy(bf16[128,256]{1,0:T(8,128)(2,1)} %step.1) | data formatting | bytes 131072

commit v3 on v2

--- a/solution.py
+++ b/solution.py
@@ -13,7 +13,7 @@
 PAIRS = 88
 SIDE = 2 * MOST + 1
 GROUP = 8
-EARLY, MIDDLE, PRE, SECOND, LATER = 1, 3, 7, 2, 0
+EARLY, MIDDLE, PRE, SECOND, LATER = 1, 2, 5, 1, 0
 MESH = pl.DeviceIdType.MESH
 
 
@@ -234,35 +234,30 @@
         message[...] = total
 
     def send_partial(layer):
-        held = [own[layer, 0]] + [line_held[layer, k] for k in range(1, across)]
-        down = jnp.dot(
-            matrix[...], jnp.concatenate(held, axis=0), preferred_element_type=jnp.float32
+        copies = []
+
+        def spread(block, held, parts, got, send, recv, target, order, blocks_out):
+            product = jnp.dot(block, jnp.concatenate(held, axis=0), preferred_element_type=jnp.float32)
+            for k in range(1, blocks_out):
+                parts[layer, k] = product[k * rows : (k + 1) * rows, :].astype(jnp.bfloat16)
+                copy = remote(
+                    parts.at[layer, k], got.at[layer, k], send.at[layer, 1, k],
+                    recv.at[layer, 1, k], target(k),
+                )
+                copy.start()
+                copies.append(copy)
+            own_field[order] = product[0:rows, :]
+
+        spread(
+            flipped[...],
+            [own[layer, 1]] + [plane_held[layer, along - k] for k in range(1, along)],
+            line_part, line_got, line_send, line_recv, lambda k: line(across - k), 1, across,
         )
-        held = [own[layer, 1]] + [plane_held[layer, along - k] for k in range(1, along)]
-        up = jnp.dot(
-            flipped[...], jnp.concatenate(held, axis=0), preferred_element_type=jnp.float32
+        spread(
+            matrix[...],
+            [own[layer, 0]] + [line_held[layer, k] for k in range(1, across)],
+            plane_part, plane_got, plane_send, plane_recv, plane, 0, along,
         )
-        copies = []
-        for k in range(1, across):
-            line_part[layer, k] = up[k * rows : (k + 1) * rows, :].astype(jnp.bfloat16)
-            copies.append(
-                remote(
-                    line_part.at[layer, k], line_got.at[layer, k], line_send.at[layer, 1, k],
-                    line_recv.at[layer, 1, k], line(across - k),
-                )
-            )
-        for k in range(1, along):
-            plane_part[layer, k] = down[k * rows : (k + 1) * rows, :].astype(jnp.bfloat16)
-            copies.append(
-                remote(
-                    plane_part.at[layer, k], plane_got.at[layer, k], plane_send.at[layer, 1, k],
-                    plane_recv.at[layer, 1, k], plane(k),
-                )
-            )
-        for copy in copies:
-            copy.start()
-        own_field[0] = down[0:rows, :]
-        own_field[1] = up[0:rows, :]
         return copies
 
     def update(layer):
@@ -309,11 +304,11 @@
         load.wait()
     pl.semaphore_wait(barrier, len(peers))
     placed_plane = [
-        remote(fractional, target_x.at[k], place_send.at[1, k], place_recv.at[1, k], plane(k))
+        remote(target_x.at[0], target_x.at[k], place_send.at[1, k], place_recv.at[1, k], plane(k))
         for k in range(1, along)
     ]
     placed_line = [
-        remote(fractional, source_x.at[k], place_send.at[0, k], place_recv.at[0, k], line(k))
+        remote(source_x.at[0], source_x.at[k], place_send.at[0, k], place_recv.at[0, k], line(k))
         for k in range(1, across)
     ]
     for copy in placed_line + placed_plane:
@@ -341,6 +336,8 @@
     fill(0, PRE)
 
     def lanes(k):
+        if isinstance(k, int):
+            return pl.ds(k * rows, rows)
         return pl.ds(pl.multiple_of(k * rows, rows), rows)
 
     def sources(k, carry):
@@ -359,10 +356,16 @@
     target_t[...] = target_rows[...].T
     for copy in placed_line:
         copy.wait_recv()
-    lax.fori_loop(1, across, sources, 0)
-    product = jnp.dot(target_t[...], source_rows[...], preferred_element_type=jnp.float32)
-    matrix[...] = product.astype(jnp.bfloat16)
-    flipped[...] = product.T.astype(jnp.bfloat16)
+    middle = max(across // 2, 1)
+    for first, last in ((0, middle), (middle, across)):
+        for k in range(max(first, 1), last):
+            sources(k, 0)
+        product = jnp.dot(
+            target_t[...], source_rows[:, first * rows : last * rows],
+            preferred_element_type=jnp.float32,
+        )
+        matrix[:, first * rows : last * rows] = product.astype(jnp.bfloat16)
+        flipped[first * rows : last * rows, :] = product.T.astype(jnp.bfloat16)
 
     sent = placed_line + placed_plane
     for layer in range(layers):
@@ -434,7 +437,7 @@
     ]
     return pl.pallas_call(
         functools.partial(step_kernel, (across, along), scale),
-        out_shape=jax.ShapeDtypeStruct(features.shape, features.dtype),
+        out_shape=pltpu.VMEM(features.shape, features.dtype),
         in_specs=[pl.BlockSpec(memory_space=pl.ANY)] * 11,
         out_specs=pl.BlockSpec(memory_space=pltpu.VMEM),
         scratch_shapes=scratch,

time: 31.6 us -> 29.7 us (0.940)
  Pallas kernels: 29.9 us -> 29 us
  local copies, waits for them, and re-layouts: 1.47 us -> 0.63 us
    pallas_call x1, Pallas kernels: 29.9 us -> 29 us  [per_device(): pl.pallas_call(functools.partial(step_kernel, (across, along), scale), ou...]
    unnamed x1, local copies, waits for them, and re-layouts: 1.47 us -> 0.63 us
where the time goes in v3:
time: 29.7 us; the launch traced here: 29.6 us
  Pallas kernels  29 us (98%)
  local copies, waits for them, and re-layouts  0.63 us (2%)
    pallas_call x1, Pallas kernels, per_device(): pl.pallas_call(functools.partial(step_kernel, (across, along), scale), ou...  29 us
    unnamed x1, local copies, waits for them, and re-layouts  0.63 us

profile of v3, /device:TPU:0, one launch (start us, length us, event | category | flops | bytes accessed | tf_op | source)
XLA Modules:
  0.0 29.6 jit_solution(1753239896408402261)
XLA Ops:
  0.0 29.0 %step.1 = bf16[128,256]{1,0:T(8,128)(2,1)S(1)} custom-call(bf16[128,256]{1,0:T(8,128)(2,1)} %features.1, f32[3,128]{1,0:T(4,128)} %fractional.1, f32[64,128]{1,0:T(8,128)} %distances.1, s32[64,128]{1,0:T(8,128)} %neighbours.1, s32[64,128]{1,0:T(8,128)} %edge_mask.1, s32[3,2048]{1,0:T(4,128)} %wave_index.1, bf16[2,64,512]{2,1,0:T(8,128)(2,1)} %w_rbf.1, ...), custom_call_target="tpu_custom_call" | custom-call | tf_op jit(solution)/shard_map/step/pallas_call | solution.py:438
  29.0 0.6 %copy.13 = bf16[128,256]{1,0:T(8,128)(2,1)} copy(bf16[128,256]{1,0:T(8,128)(2,1)S(1)} %step.1) | data formatting | bytes 131072

commit v4 on v3

--- a/solution.py
+++ b/solution.py
@@ -13,7 +13,7 @@
 PAIRS = 88
 SIDE = 2 * MOST + 1
 GROUP = 8
-EARLY, MIDDLE, PRE, SECOND, LATER = 1, 2, 5, 1, 0
+EARLY, MIDDLE, PRE, SECOND, LATER, TURN = 1, 3, 5, 0, 3, 3
 MESH = pl.DeviceIdType.MESH
 
 
@@ -233,8 +233,9 @@
                 total = total + gathered[:, at * rows : (at + 1) * rows] * factor
         message[...] = total
 
-    def send_partial(layer):
+    def send_partial(layer, far):
         copies = []
+        far_line, far_plane = far[: across - 1], far[across - 1 :]
 
         def spread(block, held, parts, got, send, recv, target, order, blocks_out):
             product = jnp.dot(block, jnp.concatenate(held, axis=0), preferred_element_type=jnp.float32)
@@ -248,11 +249,17 @@
                 copies.append(copy)
             own_field[order] = product[0:rows, :]
 
+        for copy in far_plane:
+            copy.wait_recv()
         spread(
             flipped[...],
             [own[layer, 1]] + [plane_held[layer, along - k] for k in range(1, along)],
             line_part, line_got, line_send, line_recv, lambda k: line(across - k), 1, across,
         )
+        if layer > 0:
+            fill(layer, blocks)
+        for copy in far_line:
+            copy.wait_recv()
         spread(
             matrix[...],
             [own[layer, 0]] + [line_held[layer, k] for k in range(1, across)],
@@ -373,20 +380,20 @@
         if layer > 0:
             fill(layer, min(done[layer] + LATER, blocks))
             start_near(near, cross)
-            fill(layer, blocks)
-        for copy in far:
-            copy.wait_recv()
-        copies = send_partial(layer)
+            fill(layer, min(done[layer] + TURN, blocks))
+        copies = send_partial(layer, far)
         fill(layer, blocks)
         wait_near(near, cross)
         fill_table(layer)
         gather(layer, 0, blocks)
         fill(layer + 1, SECOND)
+        for copy in sent + far:
+            copy.wait_send()
+        end_near(near, cross)
+        sent = copies
         for copy in copies:
             copy.wait_recv()
-        sent += far + copies
         state = update(layer)
-        end_near(near, cross)
         if layer + 1 < layers:
             own[layer + 1, 0] = state[:, 0:half]
             own[layer + 1, 1] = state[:, half:width]

time: 29.7 us -> 28.7 us (0.966)
  Pallas kernels: 29 us -> 27.9 us
    pallas_call x1, Pallas kernels: 29 us -> 27.9 us  [per_device(): pl.pallas_call(functools.partial(step_kernel, (across, along), scale), ou...]
where the time goes in v4:
time: 28.7 us; the launch traced here: 28.5 us
  Pallas kernels  27.9 us (97%)
  local copies, waits for them, and re-layouts  0.63 us (2%)
    pallas_call x1, Pallas kernels, per_device(): pl.pallas_call(functools.partial(step_kernel, (across, along), scale), ou...  27.9 us
    unnamed x1, local copies, waits for them, and re-layouts  0.63 us

profile of v4, /device:TPU:0, one launch (start us, length us, event | category | flops | bytes accessed | tf_op | source)
XLA Modules:
  0.0 28.5 jit_solution(4757233328666830106)
XLA Ops:
  0.0 27.9 %step.1 = bf16[128,256]{1,0:T(8,128)(2,1)S(1)} custom-call(bf16[128,256]{1,0:T(8,128)(2,1)} %features.1, f32[3,128]{1,0:T(4,128)} %fractional.1, f32[64,128]{1,0:T(8,128)} %distances.1, s32[64,128]{1,0:T(8,128)} %neighbours.1, s32[64,128]{1,0:T(8,128)} %edge_mask.1, s32[3,2048]{1,0:T(4,128)} %wave_index.1, bf16[2,64,512]{2,1,0:T(8,128)(2,1)} %w_rbf.1, ...), custom_call_target="tpu_custom_call" | custom-call | tf_op jit(solution)/shard_map/step/pallas_call | solution.py:445
  27.9 0.6 %copy.13 = bf16[128,256]{1,0:T(8,128)(2,1)} copy(bf16[128,256]{1,0:T(8,128)(2,1)S(1)} %step.1) | data formatting | bytes 131072

commit v5 on v4

--- a/solution.py
+++ b/solution.py
@@ -166,7 +166,7 @@
                     near_recv.at[layer, at, part], index,
                 )
                 (cross if part else near).append(copy)
-        for copy in far:
+        for copy in far[across - 1 :] + far[: across - 1]:
             copy.start()
         return near, cross, far
 
@@ -281,13 +281,15 @@
         state = jnp.concatenate([own[layer, 0], own[layer, 1]], axis=1).astype(jnp.float32)
         return (state + step * jax.nn.sigmoid(step)).astype(jnp.bfloat16)
 
-    def fill_table(layer):
-        def put(at, part, ref):
-            table[part * half : (part + 1) * half, at * rows : (at + 1) * rows] = transposed(ref[...])
-
-        put(0, 0, beside.at[layer, 0, 0])
+    def put(at, part, ref):
+        table[part * half : (part + 1) * half, at * rows : (at + 1) * rows] = transposed(ref[...])
+
+    def own_table(layer):
         put(1, 0, own.at[layer, 0])
         put(1, 1, own.at[layer, 1])
+
+    def fill_table(layer):
+        put(0, 0, beside.at[layer, 0, 0])
         put(2, 0, beside.at[layer, 1, 0])
         for at, slot in ((0, 1 % along), (1, along - 1)):
             pl.when(takes[at])(functools.partial(put, 2 * at, 1, beside.at[layer, at, 1]))
@@ -383,6 +385,7 @@
             fill(layer, min(done[layer] + TURN, blocks))
         copies = send_partial(layer, far)
         fill(layer, blocks)
+        own_table(layer)
         wait_near(near, cross)
         fill_table(layer)
         gather(layer, 0, blocks)

time: 28.7 us -> 28.7 us (level)
  no operation moved by 1% of the time
where the time goes in v5:
time: 28.7 us; the launch traced here: 28.5 us
  Pallas kernels  27.9 us (97%)
  local copies, waits for them, and re-layouts  0.63 us (2%)
    pallas_call x1, Pallas kernels, per_device(): pl.pallas_call(functools.partial(step_kernel, (across, along), scale), ou...  27.9 us
    unnamed x1, local copies, waits for them, and re-layouts  0.63 us

profile of v5, /device:TPU:0, one launch (start us, length us, event | category | flops | bytes accessed | tf_op | source)
XLA Modules:
  0.0 28.5 jit_solution(15085325588691191869)
XLA Ops:
  0.0 27.9 %step.1 = bf16[128,256]{1,0:T(8,128)(2,1)S(1)} custom-call(bf16[128,256]{1,0:T(8,128)(2,1)} %features.1, f32[3,128]{1,0:T(4,128)} %fractional.1, f32[64,128]{1,0:T(8,128)} %distances.1, s32[64,128]{1,0:T(8,128)} %neighbours.1, s32[64,128]{1,0:T(8,128)} %edge_mask.1, s32[3,2048]{1,0:T(4,128)} %wave_index.1, bf16[2,64,512]{2,1,0:T(8,128)(2,1)} %w_rbf.1, ...), custom_call_target="tpu_custom_call" | custom-call | tf_op jit(solution)/shard_map/step/pallas_call | solution.py:448
  27.9 0.6 %copy.13 = bf16[128,256]{1,0:T(8,128)(2,1)} copy(bf16[128,256]{1,0:T(8,128)(2,1)S(1)} %step.1) | data formatting | bytes 131072
